TPU v7x, 32 devices: a whole 2x2x4 slice. The times are simulated.
32 devices in a mesh: layer: 4 (over z), row: 2 (over x), col: 4 (over y, core).
Axes of the slice: x: 2, y: 2, z: 4, core: 2. Of those that a mesh axis runs over, the one named last changes fastest.
Arguments:
- cost_vector: float32 [8, 1024, 512], P('layer', 'row', 'col'), may hold values from -12 to 12
- metal_density: float32 [8, 1024, 512], P('layer', 'row', 'col'), may hold values from 0 to 0.5
- cap_class: int32 [8, 1024, 512], P('layer', 'row', 'col'), may hold values from 0 to 7
- blocked_mask: int32 [8, 1024, 512], P('layer', 'row', 'col'), may hold values 0 or 1
- fill_start: float32 [8, 1024, 512], P('layer', 'row', 'col'), may hold values from 0 to 1
- window_dual: float32 [8, 1024, 512], P('layer', 'row', 'col'), may hold values from -4 to 4
- layer_dual: float32 [8, 1024, 512], P('layer', 'row', 'col'), may hold values from -4 to 4
Outputs:
- fill_level: float32 [8, 1024, 512], P('layer', 'row', 'col')
- window_price: float32 [8, 1024, 512], P('layer', 'row', 'col')
- layer_price: float32 [8, 1024, 512], P('layer', 'row', 'col')
- primal_weight: float32 [], replicated
All inputs are finite; a program needn't handle non-finite values. No bound on the sum of `blocked_mask` on one device may be relied on, other than what follows from the above.
Results may differ from a plain program's by a relative error of at most 0.00011.
Values sent between devices are 32-bit elements; how exact they have to be, the bound alone decides.
A program may use at most 64 MiB of HBM per device.

v0:
```python
import jax
import jax.numpy as jnp
from jax import lax
from jax.sharding import PartitionSpec as P

WIN = 50
CAP_LEVELS = 8
ITERS = 3
step_eta = 0.4
low_density = 0.35
high_density = 0.65
layer_gap = 0.15
tiny_term = 1e-06


def extended(cells, sides, width):
    for axis, dim in sides:
        count = lax.axis_size(axis)
        ends = count - 1
        head = lax.slice_in_dim(cells, 0, width, axis=dim)
        tail = lax.slice_in_dim(cells, cells.shape[dim] - width, cells.shape[dim], axis=dim)
        cells = jnp.concatenate(
            [
                lax.ppermute(tail, axis, [(i, (i + 1) % count) for i in range(ends)]),
                cells,
                lax.ppermute(head, axis, [((i + 1) % count, i) for i in range(ends)]),
            ],
            axis=dim,
        )
    return cells


def from_behind(block, axis, distance):
    devices = range(lax.axis_size(axis))
    route = [(i - distance, i) for i in devices if i - distance in devices]
    return lax.ppermute(block, axis, route)


def band_matrix(extent_out, extent_in, offset):
    index_out = lax.broadcasted_iota(jnp.int32, (extent_out, extent_in), 0)
    index_in = lax.broadcasted_iota(jnp.int32, (extent_out, extent_in), 1)
    spread = index_in - index_out
    return ((spread >= offset) & (spread < offset + WIN)).astype(jnp.float32)


def rows_pass(row_band, padded):
    return jnp.einsum("ip,lpq->liq", row_band, padded, precision=lax.Precision.HIGHEST)


def cols_pass(partial_sum, col_band):
    return jnp.einsum("liq,qj->lij", partial_sum, col_band, precision=lax.Precision.HIGHEST)


def fill_window(level, row_band, col_band, halfway):
    tall = extended(level, (("row", 1),), halfway)
    partial_sum = rows_pass(row_band, tall)
    wide = extended(partial_sum, (("col", 2),), halfway)
    result = cols_pass(wide, col_band)
    return result


def dual_window(density_dual, row_band, col_band, halfway):
    tall = extended(density_dual, (("row", 1),), halfway)
    partial_sum = rows_pass(row_band, tall)
    wide = extended(partial_sum, (("col", 2),), halfway)
    result = cols_pass(wide, col_band)
    return result


def local(cost_vector, metal_density, cap_class, blocked_mask, fill_start, window_dual, layer_dual):
    layers_here, row_count, col_count = fill_start.shape
    halfway = WIN // 2
    inverse_area = 1.0 / (WIN * WIN)
    row_forward = band_matrix(row_count, row_count + 2 * halfway, 0)
    row_backward = band_matrix(row_count, row_count + 2 * halfway, 1)
    col_forward = band_matrix(col_count, col_count + 2 * halfway, 0).T
    col_backward = band_matrix(col_count, col_count + 2 * halfway, 1).T
    layer_ids = lax.axis_index("layer") * layers_here + lax.iota(jnp.int32, layers_here)
    keep_mask = (layer_ids < lax.axis_size("layer") * layers_here - 1).astype(jnp.float32)[
        :, None, None
    ]
    capacity = jnp.where(blocked_mask == 1, 0.0, (cap_class + 1).astype(jnp.float32) / CAP_LEVELS)
    has_floor = blocked_mask == 0
    filling = fill_start
    density_dual = window_dual
    stacked_dual = layer_dual * keep_mask
    weight = jnp.float32(1.0)
    for iteration in range(ITERS):
        primal_step = step_eta / weight
        dual_step = step_eta * weight
        below = from_behind(stacked_dual[layers_here - 1 :], "layer", 1)
        earlier = jnp.concatenate([below, stacked_dual[: layers_here - 1]], axis=0)
        transposed = dual_window(density_dual, row_backward, col_backward, halfway)
        gradient = cost_vector + transposed * inverse_area + (stacked_dual - earlier)
        fill_new = jnp.clip(filling - primal_step * gradient, 0.0, capacity)
        moved = fill_new - filling
        primal_sum = jnp.sum(moved * moved)
        level = fill_new + moved + metal_density
        above = from_behind(level[0:1], "layer", -1)
        later = jnp.concatenate([level[1:], above], axis=0)
        forward = fill_window(level, row_forward, col_forward, halfway)
        window_term = density_dual / dual_step + forward * inverse_area
        capped = jnp.minimum(window_term, high_density)
        clipped = jnp.where(has_floor, jnp.maximum(capped, low_density), capped)
        density_new = dual_step * (window_term - clipped)
        layer_term = stacked_dual / dual_step + keep_mask * (level - later)
        stacked_new = (
            dual_step * (layer_term - jnp.clip(layer_term, -layer_gap, layer_gap)) * keep_mask
        )
        density_move = density_new - density_dual
        stacked_move = stacked_new - stacked_dual
        dual_sum = jnp.sum(density_move * density_move) + jnp.sum(stacked_move * stacked_move)
        primal_sum, dual_sum = lax.psum((primal_sum, dual_sum), ("layer", "row", "col"))
        weight = jnp.sqrt(weight) * jnp.sqrt(
            jnp.sqrt((dual_sum + tiny_term) / (primal_sum + tiny_term))
        )
        filling = fill_new
        density_dual = density_new
        stacked_dual = stacked_new
    return (filling, density_dual, stacked_dual, weight)


def solution(mesh):
    in_specs = (
        P("layer", "row", "col"),
        P("layer", "row", "col"),
        P("layer", "row", "col"),
        P("layer", "row", "col"),
        P("layer", "row", "col"),
        P("layer", "row", "col"),
        P("layer", "row", "col"),
    )
    out_specs = (P("layer", "row", "col"), P("layer", "row", "col"), P("layer", "row", "col"), P())
    return jax.shard_map(local, mesh=mesh, in_specs=in_specs, out_specs=out_specs, check_vma=False)
```

profile of v0, /device:TPU:0, one launch (start us, length us, event | category | flops | bytes accessed | tf_op | source)
XLA Modules:
  0.0 268.0 jit_solution(12571616555059935040)
XLA Ops:
  1.4 4.9 %collective-permute-start = (f32[2,25,128]{2,1,0:T(8,128)S(1)}, f32[2,25,128]{2,1,0:T(8,128)S(1)}, u32[]{:S(2)}, u32[]{:S(2)}) collective-permute-start(f32[2,25,128]{2,1,0:T(8,128)S(1)} %get-tuple-element.56), channel_id=1, source_target_pairs={{0,4},{1,5},{2,6},{3,7},{8,12},{9,13},{10,14},{11,15},{16,20},{17,... | collective-permute-start | bytes 76808 | tf_op jit(solution)/shard_map/ppermute | solution.py:24
  8.8 3.6 %collective-permute-start.4 = (f32[1,512,128]{2,1,0:T(8,128)S(1)}, f32[1,512,128]{2,1,0:T(8,128)S(1)}, u32[]{:S(2)}, u32[]{:S(2)}) collective-permute-start(f32[1,512,128]{2,1,0:T(8,128)S(1)} %get-tuple-element.52), channel_id=1, source_target_pairs={{0,8},{8,16},{16,24},{1,9},{9,17},{17,25},{2,10},{10,18},{18,26},{... | collective-permute-start | bytes 786440 | tf_op jit(solution)/shard_map/ppermute | solution.py:36
  16.2 3.7 %collective-permute-done.3 = f32[2,512,25]{1,2,0:T(8,128)S(1)} collective-permute-done((f32[2,512,25]{1,2,0:T(8,128)S(1)}, f32[2,512,25]{1,2,0:T(8,128)S(1)}, u32[]{:S(2)}, u32[]{:S(2)}) %collective-permute-start.3) | collective-permute-done | bytes 102432 | tf_op jit(solution)/shard_map/ppermute | solution.py:26
  20.0 2.5 multiply_reduce_fusion.6
  22.5 4.5 %collective-permute-start.5 = (f32[2,25,128]{2,1,0:T(8,128)S(1)}, f32[2,25,128]{2,1,0:T(8,128)S(1)}, u32[]{:S(2)}, u32[]{:S(2)}) collective-permute-start(f32[2,25,128]{2,1,0:T(8,128)S(1)} %get-tuple-element.50), channel_id=1, source_target_pairs={{0,4},{1,5},{2,6},{3,7},{8,12},{9,13},{10,14},{11,15},{16,20},{17,... | collective-permute-start | bytes 76808 | tf_op jit(solution)/shard_map/ppermute | solution.py:24
  28.6 4.2 %collective-permute-done.6 = f32[2,25,128]{2,1,0:T(8,128)S(1)} collective-permute-done((f32[2,25,128]{2,1,0:T(8,128)S(1)}, f32[2,25,128]{2,1,0:T(8,128)S(1)}, u32[]{:S(2)}, u32[]{:S(2)}) %collective-permute-start.6) | collective-permute-done | bytes 25632 | tf_op jit(solution)/shard_map/ppermute | solution.py:26
  33.8 4.0 %collective-permute-start.7 = (f32[2,512,25]{1,2,0:T(8,128)S(1)}, f32[2,512,25]{1,2,0:T(8,128)S(1)}, u32[]{:S(2)}, u32[]{:S(2)}) collective-permute-start(f32[2,512,25]{1,2,0:T(8,128)S(1)} %get-tuple-element.48), channel_id=1, source_target_pairs={{0,1},{1,2},{2,3},{4,5},{5,6},{6,7},{8,9},{9,10},{10,11},{12,13},{... | collective-permute-start | bytes 307208 | tf_op jit(solution)/shard_map/ppermute | solution.py:24
  46.8 4.2 %collective-permute-done.11 = f32[2,25,128]{2,1,0:T(8,128)S(1)} collective-permute-done((f32[2,25,128]{2,1,0:T(8,128)S(1)}, f32[2,25,128]{2,1,0:T(8,128)S(1)}, u32[]{:S(2)}, u32[]{:S(2)}) %collective-permute-start.11) | collective-permute-done | bytes 25632 | tf_op jit(solution)/shard_map/ppermute | solution.py:26
  52.9 3.5 %collective-permute-start.14 = (f32[1,512,128]{2,1,0:T(8,128)S(1)}, f32[1,512,128]{2,1,0:T(8,128)S(1)}, u32[]{:S(2)}, u32[]{:S(2)}) collective-permute-start(f32[1,512,128]{2,1,0:T(8,128)S(1)} %get-tuple-element.40), channel_id=1, source_target_pairs={{0,8},{8,16},{16,24},{1,9},{9,17},{17,25},{2,10},{10,18},{18,26},{... | collective-permute-start | bytes 786440 | tf_op jit(solution)/shard_map/ppermute | solution.py:36
  57.2 4.7 %collective-permute-start.12 = (f32[2,512,25]{1,2,0:T(8,128)}, f32[2,512,25]{1,2,0:T(8,128)}, u32[]{:S(2)}, u32[]{:S(2)}) collective-permute-start(f32[2,512,25]{1,2,0:T(8,128)} %get-tuple-element.44), channel_id=1, source_target_pairs={{0,1},{1,2},{2,3},{4,5},{5,6},{6,7},{8,9},{9,10},{10,11},{12,13},{... | collective-permute-start | bytes 307208 | tf_op jit(solution)/shard_map/ppermute | solution.py:24
  64.4 40.6 %all-reduce.2 = (f32[]{:T(128)}, f32[]{:T(128)}) all-reduce(f32[]{:T(128)S(6)} %add.115, f32[]{:T(128)} %get-tuple-element.20), channel_id=1, replica_groups=mesh['layer'=4,'row'=2,'col'=4] {'layer','row','col'}, use_global_device_ids=true, to_apply=%region_2.3 | all-reduce | flops 2 | bytes 16 | tf_op jit(solution)/shard_map/psum | solution.py:113
  107.2 3.9 %multiply_reduce_fusion.3 = (f32[]{:T(128)}, f32[2,512,128]{2,1,0:T(8,128)S(1)}, f32[2,512,128]{2,1,0:T(8,128)}) fusion(f32[2,512,128]{2,1,0:T(8,128)} %get-tuple-element.58, f32[2,512,128]{2,1,0:T(8,128)S(1)} %copy-done.1, f32[2,512,128]{2,1,0:T(8,128)S(1)} %get-tuple-element.15, f32[1,512,128]{2,1,0:T(8,128)S(1)} %get-tuple-element.41, ...), kind=kOutput, calls=%fused_computation.139 | convolution fusion | flops 282915840 | bytes 5447688 | tf_op jit(solution)/shard_map/liq,qj->lij/dot_general | solution.py:51
  111.1 4.2 %collective-permute-start.15 = (f32[2,25,128]{2,1,0:T(8,128)S(1)}, f32[2,25,128]{2,1,0:T(8,128)S(1)}, u32[]{:S(2)}, u32[]{:S(2)}) collective-permute-start(f32[2,25,128]{2,1,0:T(8,128)S(1)} %get-tuple-element.38), channel_id=1, source_target_pairs={{0,4},{1,5},{2,6},{3,7},{8,12},{9,13},{10,14},{11,15},{16,20},{17,... | collective-permute-start | bytes 76808 | tf_op jit(solution)/shard_map/ppermute | solution.py:24
  116.8 4.2 %collective-permute-done.16 = f32[2,25,128]{2,1,0:T(8,128)S(1)} collective-permute-done((f32[2,25,128]{2,1,0:T(8,128)S(1)}, f32[2,25,128]{2,1,0:T(8,128)S(1)}, u32[]{:S(2)}, u32[]{:S(2)}) %collective-permute-start.16) | collective-permute-done | bytes 25632 | tf_op jit(solution)/shard_map/ppermute | solution.py:26
  126.1 2.9 %collective-permute-done.18 = f32[2,512,25]{1,2,0:T(8,128)S(1)} collective-permute-done((f32[2,512,25]{1,2,0:T(8,128)S(1)}, f32[2,512,25]{1,2,0:T(8,128)S(1)}, u32[]{:S(2)}, u32[]{:S(2)}) %collective-permute-start.18) | collective-permute-done | bytes 102432 | tf_op jit(solution)/shard_map/ppermute | solution.py:26
  134.0 4.2 %collective-permute-done.21 = f32[2,25,128]{2,1,0:T(8,128)S(1)} collective-permute-done((f32[2,25,128]{2,1,0:T(8,128)S(1)}, f32[2,25,128]{2,1,0:T(8,128)S(1)}, u32[]{:S(2)}, u32[]{:S(2)}) %collective-permute-start.21) | collective-permute-done | bytes 25632 | tf_op jit(solution)/shard_map/ppermute | solution.py:26
  143.3 4.7 %collective-permute-start.22 = (f32[2,512,25]{1,2,0:T(8,128)}, f32[2,512,25]{1,2,0:T(8,128)}, u32[]{:S(2)}, u32[]{:S(2)}) collective-permute-start(f32[2,512,25]{1,2,0:T(8,128)} %get-tuple-element.32), channel_id=1, source_target_pairs={{0,1},{1,2},{2,3},{4,5},{5,6},{6,7},{8,9},{9,10},{10,11},{12,13},{... | collective-permute-start | bytes 307208 | tf_op jit(solution)/shard_map/ppermute | solution.py:24
  150.6 40.6 %all-reduce.1 = (f32[]{:T(128)}, f32[]{:T(128)}) all-reduce(f32[]{:T(128)S(6)} %add.124, f32[]{:T(128)} %get-tuple-element.18), channel_id=1, replica_groups=mesh['layer'=4,'row'=2,'col'=4] {'layer','row','col'}, use_global_device_ids=true, to_apply=%region_7.8 | all-reduce | flops 2 | bytes 16 | tf_op jit(solution)/shard_map/psum | solution.py:113
  193.4 3.9 %multiply_reduce_fusion = (f32[]{:T(128)}, f32[2,512,128]{2,1,0:T(8,128)S(1)}, f32[2,512,128]{2,1,0:T(8,128)}) fusion(f32[2,512,128]{2,1,0:T(8,128)} %get-tuple-element.61, f32[2,512,128]{2,1,0:T(8,128)S(1)} %copy-done.1, f32[2,512,128]{2,1,0:T(8,128)S(1)} %get-tuple-element.13, f32[1,512,128]{2,1,0:T(8,128)S(1)} %get-tuple-element.29, ...), kind=kOutput, calls=%fused_computation.134 | convolution fusion | flops 282915840 | bytes 5447688 | tf_op jit(solution)/shard_map/liq,qj->lij/dot_general | solution.py:51
  197.3 4.2 %collective-permute-start.25 = (f32[2,25,128]{2,1,0:T(8,128)S(1)}, f32[2,25,128]{2,1,0:T(8,128)S(1)}, u32[]{:S(2)}, u32[]{:S(2)}) collective-permute-start(f32[2,25,128]{2,1,0:T(8,128)S(1)} %get-tuple-element.26), channel_id=1, source_target_pairs={{0,4},{1,5},{2,6},{3,7},{8,12},{9,13},{10,14},{11,15},{16,20},{17,... | collective-permute-start | bytes 76808 | tf_op jit(solution)/shard_map/ppermute | solution.py:24
  203.1 4.2 %collective-permute-done.26 = f32[2,25,128]{2,1,0:T(8,128)S(1)} collective-permute-done((f32[2,25,128]{2,1,0:T(8,128)S(1)}, f32[2,25,128]{2,1,0:T(8,128)S(1)}, u32[]{:S(2)}, u32[]{:S(2)}) %collective-permute-start.26) | collective-permute-done | bytes 25632 | tf_op jit(solution)/shard_map/ppermute | solution.py:26
  212.4 2.9 %collective-permute-done.28 = f32[2,512,25]{1,2,0:T(8,128)S(1)} collective-permute-done((f32[2,512,25]{1,2,0:T(8,128)S(1)}, f32[2,512,25]{1,2,0:T(8,128)S(1)}, u32[]{:S(2)}, u32[]{:S(2)}) %collective-permute-start.28) | collective-permute-done | bytes 102432 | tf_op jit(solution)/shard_map/ppermute | solution.py:26
  215.3 2.5 multiply_reduce_fusion.2
  222.5 43.0 %all-reduce = (f32[]{:T(128)}, f32[]{:T(128)}) all-reduce(f32[]{:T(128)S(6)} %add.133, f32[]{:T(128)} %get-tuple-element.16), channel_id=1, replica_groups=mesh['layer'=4,'row'=2,'col'=4] {'layer','row','col'}, use_global_device_ids=true, to_apply=%region_12.13 | all-reduce | flops 2 | bytes 16 | tf_op jit(solution)/shard_map/psum | solution.py:113
  (108 shorter events, 51.4 us)
Async XLA Ops:
  1.4 11.0 %collective-permute-start = (f32[2,25,128]{2,1,0:T(8,128)S(1)}, f32[2,25,128]{2,1,0:T(8,128)S(1)}, u32[]{:S(2)}, u32[]{:S(2)}) collective-permute-start(f32[2,25,128]{2,1,0:T(8,128)S(1)} %get-tuple-element.56), channel_id=1, source_target_pairs={{0,4},{1,5},{2,6},{3,7},{8,12},{9,13},{10,14},{11,15},{16,20},{17,... | collective-permute-start | bytes 76808 | tf_op jit(solution)/shard_map/ppermute | solution.py:24
  6.3 6.2 %collective-permute-start.1 = (f32[2,25,128]{2,1,0:T(8,128)S(1)}, f32[2,25,128]{2,1,0:T(8,128)S(1)}, u32[]{:S(2)}, u32[]{:S(2)}) collective-permute-start(f32[2,25,128]{2,1,0:T(8,128)S(1)} %get-tuple-element.57), channel_id=1, source_target_pairs={{4,0},{5,1},{6,2},{7,3},{12,8},{13,9},{14,10},{15,11},{20,16},{21,... | collective-permute-start | bytes 76808 | tf_op jit(solution)/shard_map/ppermute | solution.py:26
  8.8 11.1 %collective-permute-start.4 = (f32[1,512,128]{2,1,0:T(8,128)S(1)}, f32[1,512,128]{2,1,0:T(8,128)S(1)}, u32[]{:S(2)}, u32[]{:S(2)}) collective-permute-start(f32[1,512,128]{2,1,0:T(8,128)S(1)} %get-tuple-element.52), channel_id=1, source_target_pairs={{0,8},{8,16},{16,24},{1,9},{9,17},{17,25},{2,10},{10,18},{18,26},{... | collective-permute-start | bytes 786440 | tf_op jit(solution)/shard_map/ppermute | solution.py:36
  14.9 5.0 %collective-permute-start.3 = (f32[2,512,25]{1,2,0:T(8,128)S(1)}, f32[2,512,25]{1,2,0:T(8,128)S(1)}, u32[]{:S(2)}, u32[]{:S(2)}) collective-permute-start(f32[2,512,25]{1,2,0:T(8,128)S(1)} %get-tuple-element.55), channel_id=1, source_target_pairs={{1,0},{2,1},{3,2},{5,4},{6,5},{7,6},{9,8},{10,9},{11,10},{13,12},{... | collective-permute-start | bytes 307208 | tf_op jit(solution)/shard_map/ppermute | solution.py:26
  22.5 6.1 %collective-permute-start.5 = (f32[2,25,128]{2,1,0:T(8,128)S(1)}, f32[2,25,128]{2,1,0:T(8,128)S(1)}, u32[]{:S(2)}, u32[]{:S(2)}) collective-permute-start(f32[2,25,128]{2,1,0:T(8,128)S(1)} %get-tuple-element.50), channel_id=1, source_target_pairs={{0,4},{1,5},{2,6},{3,7},{8,12},{9,13},{10,14},{11,15},{16,20},{17,... | collective-permute-start | bytes 76808 | tf_op jit(solution)/shard_map/ppermute | solution.py:24
  27.0 5.8 %collective-permute-start.6 = (f32[2,25,128]{2,1,0:T(8,128)S(1)}, f32[2,25,128]{2,1,0:T(8,128)S(1)}, u32[]{:S(2)}, u32[]{:S(2)}) collective-permute-start(f32[2,25,128]{2,1,0:T(8,128)S(1)} %get-tuple-element.51), channel_id=1, source_target_pairs={{4,0},{5,1},{6,2},{7,3},{12,8},{13,9},{14,10},{15,11},{20,16},{21,... | collective-permute-start | bytes 76808 | tf_op jit(solution)/shard_map/ppermute | solution.py:26
  33.8 6.7 %collective-permute-start.7 = (f32[2,512,25]{1,2,0:T(8,128)S(1)}, f32[2,512,25]{1,2,0:T(8,128)S(1)}, u32[]{:S(2)}, u32[]{:S(2)}) collective-permute-start(f32[2,512,25]{1,2,0:T(8,128)S(1)} %get-tuple-element.48), channel_id=1, source_target_pairs={{0,1},{1,2},{2,3},{4,5},{5,6},{6,7},{8,9},{9,10},{10,11},{12,13},{... | collective-permute-start | bytes 307208 | tf_op jit(solution)/shard_map/ppermute | solution.py:24
  39.2 12.8 %collective-permute-start.9 = (f32[1,512,128]{2,1,0:T(8,128)S(1)}, f32[1,512,128]{2,1,0:T(8,128)S(1)}, u32[]{:S(2)}, u32[]{:S(2)}) collective-permute-start(f32[1,512,128]{2,1,0:T(8,128)S(1)} %get-tuple-element.43), channel_id=1, source_target_pairs={{8,0},{16,8},{24,16},{9,1},{17,9},{25,17},{10,2},{18,10},{26,18},{... | collective-permute-start | bytes 786440 | tf_op jit(solution)/shard_map/ppermute | solution.py:36
  45.2 5.8 %collective-permute-start.11 = (f32[2,25,128]{2,1,0:T(8,128)S(1)}, f32[2,25,128]{2,1,0:T(8,128)S(1)}, u32[]{:S(2)}, u32[]{:S(2)}) collective-permute-start(f32[2,25,128]{2,1,0:T(8,128)S(1)} %get-tuple-element.47), channel_id=1, source_target_pairs={{4,0},{5,1},{6,2},{7,3},{12,8},{13,9},{14,10},{15,11},{20,16},{21,... | collective-permute-start | bytes 76808 | tf_op jit(solution)/shard_map/ppermute | solution.py:26
  52.9 53.5 %collective-permute-start.14 = (f32[1,512,128]{2,1,0:T(8,128)S(1)}, f32[1,512,128]{2,1,0:T(8,128)S(1)}, u32[]{:S(2)}, u32[]{:S(2)}) collective-permute-start(f32[1,512,128]{2,1,0:T(8,128)S(1)} %get-tuple-element.40), channel_id=1, source_target_pairs={{0,8},{8,16},{16,24},{1,9},{9,17},{17,25},{2,10},{10,18},{18,26},{... | collective-permute-start | bytes 786440 | tf_op jit(solution)/shard_map/ppermute | solution.py:36
  57.2 49.2 %collective-permute-start.12 = (f32[2,512,25]{1,2,0:T(8,128)}, f32[2,512,25]{1,2,0:T(8,128)}, u32[]{:S(2)}, u32[]{:S(2)}) collective-permute-start(f32[2,512,25]{1,2,0:T(8,128)} %get-tuple-element.44), channel_id=1, source_target_pairs={{0,1},{1,2},{2,3},{4,5},{5,6},{6,7},{8,9},{9,10},{10,11},{12,13},{... | collective-permute-start | bytes 307208 | tf_op jit(solution)/shard_map/ppermute | solution.py:24
  61.9 44.6 %collective-permute-start.13 = (f32[2,512,25]{1,2,0:T(8,128)}, f32[2,512,25]{1,2,0:T(8,128)}, u32[]{:S(2)}, u32[]{:S(2)}) collective-permute-start(f32[2,512,25]{1,2,0:T(8,128)} %get-tuple-element.45), channel_id=1, source_target_pairs={{1,0},{2,1},{3,2},{5,4},{6,5},{7,6},{9,8},{10,9},{11,10},{13,12},{... | collective-permute-start | bytes 307208 | tf_op jit(solution)/shard_map/ppermute | solution.py:26
  111.1 5.8 %collective-permute-start.15 = (f32[2,25,128]{2,1,0:T(8,128)S(1)}, f32[2,25,128]{2,1,0:T(8,128)S(1)}, u32[]{:S(2)}, u32[]{:S(2)}) collective-permute-start(f32[2,25,128]{2,1,0:T(8,128)S(1)} %get-tuple-element.38), channel_id=1, source_target_pairs={{0,4},{1,5},{2,6},{3,7},{8,12},{9,13},{10,14},{11,15},{16,20},{17,... | collective-permute-start | bytes 76808 | tf_op jit(solution)/shard_map/ppermute | solution.py:24
  115.2 5.8 %collective-permute-start.16 = (f32[2,25,128]{2,1,0:T(8,128)S(1)}, f32[2,25,128]{2,1,0:T(8,128)S(1)}, u32[]{:S(2)}, u32[]{:S(2)}) collective-permute-start(f32[2,25,128]{2,1,0:T(8,128)S(1)} %get-tuple-element.39), channel_id=1, source_target_pairs={{4,0},{5,1},{6,2},{7,3},{12,8},{13,9},{14,10},{15,11},{20,16},{21,... | collective-permute-start | bytes 76808 | tf_op jit(solution)/shard_map/ppermute | solution.py:26
  123.3 5.7 %collective-permute-start.18 = (f32[2,512,25]{1,2,0:T(8,128)S(1)}, f32[2,512,25]{1,2,0:T(8,128)S(1)}, u32[]{:S(2)}, u32[]{:S(2)}) collective-permute-start(f32[2,512,25]{1,2,0:T(8,128)S(1)} %get-tuple-element.37), channel_id=1, source_target_pairs={{1,0},{2,1},{3,2},{5,4},{6,5},{7,6},{9,8},{10,9},{11,10},{13,12},{... | collective-permute-start | bytes 307208 | tf_op jit(solution)/shard_map/ppermute | solution.py:26
  124.8 14.4 %collective-permute-start.19 = (f32[1,512,128]{2,1,0:T(8,128)S(1)}, f32[1,512,128]{2,1,0:T(8,128)S(1)}, u32[]{:S(2)}, u32[]{:S(2)}) collective-permute-start(f32[1,512,128]{2,1,0:T(8,128)S(1)} %get-tuple-element.31), channel_id=1, source_target_pairs={{8,0},{16,8},{24,16},{9,1},{17,9},{25,17},{10,2},{18,10},{26,18},{... | collective-permute-start | bytes 786440 | tf_op jit(solution)/shard_map/ppermute | solution.py:36
  132.4 5.8 %collective-permute-start.21 = (f32[2,25,128]{2,1,0:T(8,128)S(1)}, f32[2,25,128]{2,1,0:T(8,128)S(1)}, u32[]{:S(2)}, u32[]{:S(2)}) collective-permute-start(f32[2,25,128]{2,1,0:T(8,128)S(1)} %get-tuple-element.35), channel_id=1, source_target_pairs={{4,0},{5,1},{6,2},{7,3},{12,8},{13,9},{14,10},{15,11},{20,16},{21,... | collective-permute-start | bytes 76808 | tf_op jit(solution)/shard_map/ppermute | solution.py:26
  140.2 52.5 %collective-permute-start.24 = (f32[1,512,128]{2,1,0:T(8,128)S(1)}, f32[1,512,128]{2,1,0:T(8,128)S(1)}, u32[]{:S(2)}, u32[]{:S(2)}) collective-permute-start(f32[1,512,128]{2,1,0:T(8,128)S(1)} %get-tuple-element.28), channel_id=1, source_target_pairs={{0,8},{8,16},{16,24},{1,9},{9,17},{17,25},{2,10},{10,18},{18,26},{... | collective-permute-start | bytes 786440 | tf_op jit(solution)/shard_map/ppermute | solution.py:36
  143.3 49.4 %collective-permute-start.22 = (f32[2,512,25]{1,2,0:T(8,128)}, f32[2,512,25]{1,2,0:T(8,128)}, u32[]{:S(2)}, u32[]{:S(2)}) collective-permute-start(f32[2,512,25]{1,2,0:T(8,128)} %get-tuple-element.32), channel_id=1, source_target_pairs={{0,1},{1,2},{2,3},{4,5},{5,6},{6,7},{8,9},{9,10},{10,11},{12,13},{... | collective-permute-start | bytes 307208 | tf_op jit(solution)/shard_map/ppermute | solution.py:24
  148.0 44.7 %collective-permute-start.23 = (f32[2,512,25]{1,2,0:T(8,128)}, f32[2,512,25]{1,2,0:T(8,128)}, u32[]{:S(2)}, u32[]{:S(2)}) collective-permute-start(f32[2,512,25]{1,2,0:T(8,128)} %get-tuple-element.33), channel_id=1, source_target_pairs={{1,0},{2,1},{3,2},{5,4},{6,5},{7,6},{9,8},{10,9},{11,10},{13,12},{... | collective-permute-start | bytes 307208 | tf_op jit(solution)/shard_map/ppermute | solution.py:26
  197.3 5.8 %collective-permute-start.25 = (f32[2,25,128]{2,1,0:T(8,128)S(1)}, f32[2,25,128]{2,1,0:T(8,128)S(1)}, u32[]{:S(2)}, u32[]{:S(2)}) collective-permute-start(f32[2,25,128]{2,1,0:T(8,128)S(1)} %get-tuple-element.26), channel_id=1, source_target_pairs={{0,4},{1,5},{2,6},{3,7},{8,12},{9,13},{10,14},{11,15},{16,20},{17,... | collective-permute-start | bytes 76808 | tf_op jit(solution)/shard_map/ppermute | solution.py:24
  201.5 5.8 %collective-permute-start.26 = (f32[2,25,128]{2,1,0:T(8,128)S(1)}, f32[2,25,128]{2,1,0:T(8,128)S(1)}, u32[]{:S(2)}, u32[]{:S(2)}) collective-permute-start(f32[2,25,128]{2,1,0:T(8,128)S(1)} %get-tuple-element.27), channel_id=1, source_target_pairs={{4,0},{5,1},{6,2},{7,3},{12,8},{13,9},{14,10},{15,11},{20,16},{21,... | collective-permute-start | bytes 76808 | tf_op jit(solution)/shard_map/ppermute | solution.py:26
  209.5 5.7 %collective-permute-start.28 = (f32[2,512,25]{1,2,0:T(8,128)S(1)}, f32[2,512,25]{1,2,0:T(8,128)S(1)}, u32[]{:S(2)}, u32[]{:S(2)}) collective-permute-start(f32[2,512,25]{1,2,0:T(8,128)S(1)} %get-tuple-element.25), channel_id=1, source_target_pairs={{1,0},{2,1},{3,2},{5,4},{6,5},{7,6},{9,8},{10,9},{11,10},{13,12},{... | collective-permute-start | bytes 307208 | tf_op jit(solution)/shard_map/ppermute | solution.py:26
  211.0 8.6 %collective-permute-start.29 = (f32[1,512,128]{2,1,0:T(8,128)S(1)}, f32[1,512,128]{2,1,0:T(8,128)S(1)}, u32[]{:S(2)}, u32[]{:S(2)}) collective-permute-start(f32[1,512,128]{2,1,0:T(8,128)S(1)} %get-tuple-element.23), channel_id=1, source_target_pairs={{8,0},{16,8},{24,16},{9,1},{17,9},{25,17},{10,2},{18,10},{26,18},{... | collective-permute-start | bytes 786440 | tf_op jit(solution)/shard_map/ppermute | solution.py:36
  (22 other events, 157.5 us)
where the time goes:
time: 269 us; the launch traced here: 268 us
  blocking collectives  124 us (46%)
  starting transfers between devices  67.7 us (25%)
  waiting for transfers between devices  35 us (13%)
  matrix products  21.7 us (8%)
  between operations  10.6 us (4%)
  other arithmetic  4.76 us (2%)
  local copies, waits for them, and re-layouts  4.08 us (2%)
    psum x3, blocking collectives, local(): lax.psum((primal_sum, dual_sum), ('layer', 'row', 'col'))  124 us
    ppermute x12, starting transfers between devices, extended(): lax.ppermute(tail, axis, [(i, (i + 1) % count) for i in range(ends)])  38.4 us
    ppermute x12, waiting for transfers between devices, extended(): lax.ppermute(head, axis, [((i + 1) % count, i) for i in range(ends)])  32.1 us
    dot_general x6, matrix products, cols_pass(): jnp.einsum('liq,qj->lij', partial_sum, col_band, precision=lax.Precision....  16.3 us
    ppermute x12, starting transfers between devices, extended(): lax.ppermute(head, axis, [((i + 1) % count, i) for i in range(ends)])  15.9 us
    ppermute x6, starting transfers between devices, from_behind(): return lax.ppermute(block, axis, route)  13.4 us
    dot_general x6, matrix products, rows_pass(): jnp.einsum('ip,lpq->liq', row_band, padded, precision=lax.Precision.HIGHEST)  5.39 us
  transfers between devices with their start and end apart: 30, of which 15 were waited for; matrix products, arithmetic and copies ran while one was open for 4% of the time, Pallas kernels for 0%

commit v1 on v0

--- a/solution.py
+++ b/solution.py
@@ -110,7 +110,7 @@
         density_move = density_new - density_dual
         stacked_move = stacked_new - stacked_dual
         dual_sum = jnp.sum(density_move * density_move) + jnp.sum(stacked_move * stacked_move)
-        primal_sum, dual_sum = lax.psum((primal_sum, dual_sum), ("layer", "row", "col"))
+        primal_sum, dual_sum = lax.psum(lax.psum((primal_sum, dual_sum), "layer"), ("row", "col"))
         weight = jnp.sqrt(weight) * jnp.sqrt(
             jnp.sqrt((dual_sum + tiny_term) / (primal_sum + tiny_term))
         )

time: 269 us -> 211 us (0.78)
  blocking collectives: 124 us -> 69.2 us
    psum x3 -> x6, blocking collectives: 124 us -> 69.2 us  [the longest x3 38.8 us: local(): lax.psum(lax.psum((primal_sum, dual_sum), 'layer'), ('row', 'col'))]
    ppermute x6, waiting for transfers between devices: 1.77 us -> 6.5 us  [from_behind(): return lax.ppermute(block, axis, route)]
    ppermute x12, waiting for transfers between devices: 32.1 us -> 27.3 us  [extended(): lax.ppermute(head, axis, [((i + 1) % count, i) for i in range(ends)])]
    ppermute x12, starting transfers between devices: 38.4 us -> 34.4 us  [extended(): lax.ppermute(tail, axis, [(i, (i + 1) % count) for i in range(ends)])]
  transfers between devices with their start and end apart: 30 -> 30, of which waited for: 15 -> 15; matrix products, arithmetic and copies ran while one was open for 4% -> 5% of each run, Pallas kernels for 0% -> 0%
where the time goes in v1:
time: 211 us; the launch traced here: 210 us
  blocking collectives  69.2 us (33%)
  starting transfers between devices  65.4 us (31%)
  waiting for transfers between devices  35 us (17%)
  matrix products  21.7 us (10%)
  between operations  10.2 us (5%)
  other arithmetic  4.7 us (2%)
  local copies, waits for them, and re-layouts  4.03 us (2%)
    psum x3, blocking collectives, local(): lax.psum(lax.psum((primal_sum, dual_sum), 'layer'), ('row', 'col'))  38.8 us
    ppermute x12, starting transfers between devices, extended(): lax.ppermute(tail, axis, [(i, (i + 1) % count) for i in range(ends)])  34.4 us
    psum x3, blocking collectives, local(): lax.psum((primal_sum, dual_sum), 'layer')  30.4 us
    ppermute x12, waiting for transfers between devices, extended(): lax.ppermute(head, axis, [((i + 1) % count, i) for i in range(ends)])  27.3 us
    dot_general x6, matrix products, cols_pass(): jnp.einsum('liq,qj->lij', partial_sum, col_band, precision=lax.Precision....  16.3 us
    ppermute x12, starting transfers between devices, extended(): lax.ppermute(head, axis, [((i + 1) % count, i) for i in range(ends)])  15.9 us
    ppermute x6, starting transfers between devices, from_behind(): return lax.ppermute(block, axis, route)  15.1 us
    ppermute x6, waiting for transfers between devices, from_behind(): return lax.ppermute(block, axis, route)  6.5 us
  transfers between devices with their start and end apart: 30, of which 15 were waited for; matrix products, arithmetic and copies ran while one was open for 5% of the time, Pallas kernels for 0%

profile of v1, /device:TPU:0, one launch (start us, length us, event | category | flops | bytes accessed | tf_op | source)
XLA Modules:
  0.0 210.2 jit_solution(7210298670685279767)
XLA Ops:
  1.4 4.9 %collective-permute-start = (f32[2,25,128]{2,1,0:T(8,128)S(1)}, f32[2,25,128]{2,1,0:T(8,128)S(1)}, u32[]{:S(2)}, u32[]{:S(2)}) collective-permute-start(f32[2,25,128]{2,1,0:T(8,128)S(1)} %get-tuple-element.62), channel_id=1, source_target_pairs={{0,4},{1,5},{2,6},{3,7},{8,12},{9,13},{10,14},{11,15},{16,20},{17,... | collective-permute-start | bytes 76808 | tf_op jit(solution)/shard_map/ppermute | solution.py:24
  8.8 3.6 %collective-permute-start.4 = (f32[1,512,128]{2,1,0:T(8,128)S(1)}, f32[1,512,128]{2,1,0:T(8,128)S(1)}, u32[]{:S(2)}, u32[]{:S(2)}) collective-permute-start(f32[1,512,128]{2,1,0:T(8,128)S(1)} %get-tuple-element.58), channel_id=1, source_target_pairs={{0,8},{8,16},{16,24},{1,9},{9,17},{17,25},{2,10},{10,18},{18,26},{... | collective-permute-start | bytes 786440 | tf_op jit(solution)/shard_map/ppermute | solution.py:36
  16.2 3.7 %collective-permute-done.3 = f32[2,512,25]{1,2,0:T(8,128)S(1)} collective-permute-done((f32[2,512,25]{1,2,0:T(8,128)S(1)}, f32[2,512,25]{1,2,0:T(8,128)S(1)}, u32[]{:S(2)}, u32[]{:S(2)}) %collective-permute-start.3) | collective-permute-done | bytes 102432 | tf_op jit(solution)/shard_map/ppermute | solution.py:26
  22.5 4.5 %collective-permute-start.5 = (f32[2,25,128]{2,1,0:T(8,128)S(1)}, f32[2,25,128]{2,1,0:T(8,128)S(1)}, u32[]{:S(2)}, u32[]{:S(2)}) collective-permute-start(f32[2,25,128]{2,1,0:T(8,128)S(1)} %get-tuple-element.56), channel_id=1, source_target_pairs={{0,4},{1,5},{2,6},{3,7},{8,12},{9,13},{10,14},{11,15},{16,20},{17,... | collective-permute-start | bytes 76808 | tf_op jit(solution)/shard_map/ppermute | solution.py:24
  28.6 4.2 %collective-permute-done.6 = f32[2,25,128]{2,1,0:T(8,128)S(1)} collective-permute-done((f32[2,25,128]{2,1,0:T(8,128)S(1)}, f32[2,25,128]{2,1,0:T(8,128)S(1)}, u32[]{:S(2)}, u32[]{:S(2)}) %collective-permute-start.6) | collective-permute-done | bytes 25632 | tf_op jit(solution)/shard_map/ppermute | solution.py:26
  33.8 4.0 %collective-permute-start.7 = (f32[2,512,25]{1,2,0:T(8,128)S(1)}, f32[2,512,25]{1,2,0:T(8,128)S(1)}, u32[]{:S(2)}, u32[]{:S(2)}) collective-permute-start(f32[2,512,25]{1,2,0:T(8,128)S(1)} %get-tuple-element.54), channel_id=1, source_target_pairs={{0,1},{1,2},{2,3},{4,5},{5,6},{6,7},{8,9},{9,10},{10,11},{12,13},{... | collective-permute-start | bytes 307208 | tf_op jit(solution)/shard_map/ppermute | solution.py:24
  46.8 4.2 %collective-permute-done.11 = f32[2,25,128]{2,1,0:T(8,128)S(1)} collective-permute-done((f32[2,25,128]{2,1,0:T(8,128)S(1)}, f32[2,25,128]{2,1,0:T(8,128)S(1)}, u32[]{:S(2)}, u32[]{:S(2)}) %collective-permute-start.11) | collective-permute-done | bytes 25632 | tf_op jit(solution)/shard_map/ppermute | solution.py:26
  52.9 3.5 %collective-permute-start.14 = (f32[1,512,128]{2,1,0:T(8,128)S(1)}, f32[1,512,128]{2,1,0:T(8,128)S(1)}, u32[]{:S(2)}, u32[]{:S(2)}) collective-permute-start(f32[1,512,128]{2,1,0:T(8,128)S(1)} %get-tuple-element.46), channel_id=1, source_target_pairs={{0,8},{8,16},{16,24},{1,9},{9,17},{17,25},{2,10},{10,18},{18,26},{... | collective-permute-start | bytes 786440 | tf_op jit(solution)/shard_map/ppermute | solution.py:36
  57.1 4.7 %collective-permute-start.12 = (f32[2,512,25]{1,2,0:T(8,128)}, f32[2,512,25]{1,2,0:T(8,128)}, u32[]{:S(2)}, u32[]{:S(2)}) collective-permute-start(f32[2,512,25]{1,2,0:T(8,128)} %get-tuple-element.50), channel_id=1, source_target_pairs={{0,1},{1,2},{2,3},{4,5},{5,6},{6,7},{8,9},{9,10},{10,11},{12,13},{... | collective-permute-start | bytes 307208 | tf_op jit(solution)/shard_map/ppermute | solution.py:24
  64.3 10.6 %all-reduce.5 = (f32[]{:T(128)}, f32[]{:T(128)}) all-reduce(f32[]{:T(128)S(6)} %add.127, f32[]{:T(128)} %get-tuple-element.26), channel_id=1, replica_groups=mesh['layer'=4,'row'=2,'col'=4] {'layer'}, use_global_device_ids=true, to_apply=%region_2.3 | all-reduce | flops 2 | bytes 16 | tf_op jit(solution)/shard_map/psum | solution.py:113
  75.0 12.4 %all-reduce.2 = (f32[]{:T(128)}, f32[]{:T(128)}) all-reduce(f32[]{:T(128)} %get-tuple-element.14, f32[]{:T(128)} %get-tuple-element.15), channel_id=1, replica_groups=mesh['layer'=4,'row'=2,'col'=4] {'row','col'}, use_global_device_ids=true, to_apply=%region_3.4 | all-reduce | flops 2 | bytes 16 | tf_op jit(solution)/shard_map/psum | solution.py:113
  89.5 3.9 %multiply_reduce_fusion.3 = (f32[]{:T(128)}, f32[2,512,128]{2,1,0:T(8,128)S(1)}, f32[2,512,128]{2,1,0:T(8,128)}) fusion(f32[2,512,128]{2,1,0:T(8,128)} %get-tuple-element.64, f32[2,512,128]{2,1,0:T(8,128)S(1)} %copy-done.1, f32[2,512,128]{2,1,0:T(8,128)S(1)} %get-tuple-element.21, f32[1,512,128]{2,1,0:T(8,128)S(1)} %get-tuple-element.47, ...), kind=kOutput, calls=%fused_computation.139 | convolution fusion | flops 282915840 | bytes 5447688 | tf_op jit(solution)/shard_map/liq,qj->lij/dot_general | solution.py:51
  93.4 3.2 %collective-permute-start.15 = (f32[2,25,128]{2,1,0:T(8,128)S(1)}, f32[2,25,128]{2,1,0:T(8,128)S(1)}, u32[]{:S(2)}, u32[]{:S(2)}) collective-permute-start(f32[2,25,128]{2,1,0:T(8,128)S(1)} %get-tuple-element.44), channel_id=1, source_target_pairs={{0,4},{1,5},{2,6},{3,7},{8,12},{9,13},{10,14},{11,15},{16,20},{17,... | collective-permute-start | bytes 76808 | tf_op jit(solution)/shard_map/ppermute | solution.py:24
  98.2 4.2 %collective-permute-done.16 = f32[2,25,128]{2,1,0:T(8,128)S(1)} collective-permute-done((f32[2,25,128]{2,1,0:T(8,128)S(1)}, f32[2,25,128]{2,1,0:T(8,128)S(1)}, u32[]{:S(2)}, u32[]{:S(2)}) %collective-permute-start.16) | collective-permute-done | bytes 25632 | tf_op jit(solution)/shard_map/ppermute | solution.py:26
  113.0 4.2 %collective-permute-done.21 = f32[2,25,128]{2,1,0:T(8,128)S(1)} collective-permute-done((f32[2,25,128]{2,1,0:T(8,128)S(1)}, f32[2,25,128]{2,1,0:T(8,128)S(1)}, u32[]{:S(2)}, u32[]{:S(2)}) %collective-permute-start.21) | collective-permute-done | bytes 25632 | tf_op jit(solution)/shard_map/ppermute | solution.py:26
  119.1 4.1 %collective-permute-start.24 = (f32[1,512,128]{2,1,0:T(8,128)S(1)}, f32[1,512,128]{2,1,0:T(8,128)S(1)}, u32[]{:S(2)}, u32[]{:S(2)}) collective-permute-start(f32[1,512,128]{2,1,0:T(8,128)S(1)} %get-tuple-element.34), channel_id=1, source_target_pairs={{0,8},{8,16},{16,24},{1,9},{9,17},{17,25},{2,10},{10,18},{18,26},{... | collective-permute-start | bytes 786440 | tf_op jit(solution)/shard_map/ppermute | solution.py:36
  129.1 9.3 %all-reduce.4 = (f32[]{:T(128)}, f32[]{:T(128)}) all-reduce(f32[]{:T(128)S(6)} %add.136, f32[]{:T(128)} %get-tuple-element.24), channel_id=1, replica_groups=mesh['layer'=4,'row'=2,'col'=4] {'layer'}, use_global_device_ids=true, to_apply=%region_9.10 | all-reduce | flops 2 | bytes 16 | tf_op jit(solution)/shard_map/psum | solution.py:113
  138.4 14.0 %all-reduce.1 = (f32[]{:T(128)}, f32[]{:T(128)}) all-reduce(f32[]{:T(128)} %get-tuple-element.12, f32[]{:T(128)} %get-tuple-element.13), channel_id=1, replica_groups=mesh['layer'=4,'row'=2,'col'=4] {'row','col'}, use_global_device_ids=true, to_apply=%region_10.11 | all-reduce | flops 2 | bytes 16 | tf_op jit(solution)/shard_map/psum | solution.py:113
  154.5 3.9 %multiply_reduce_fusion = (f32[]{:T(128)}, f32[2,512,128]{2,1,0:T(8,128)S(1)}, f32[2,512,128]{2,1,0:T(8,128)}) fusion(f32[2,512,128]{2,1,0:T(8,128)} %get-tuple-element.67, f32[2,512,128]{2,1,0:T(8,128)S(1)} %copy-done.1, f32[2,512,128]{2,1,0:T(8,128)S(1)} %get-tuple-element.19, f32[1,512,128]{2,1,0:T(8,128)S(1)} %get-tuple-element.35, ...), kind=kOutput, calls=%fused_computation.134 | convolution fusion | flops 282915840 | bytes 5447688 | tf_op jit(solution)/shard_map/liq,qj->lij/dot_general | solution.py:51
  158.4 3.2 %collective-permute-start.25 = (f32[2,25,128]{2,1,0:T(8,128)S(1)}, f32[2,25,128]{2,1,0:T(8,128)S(1)}, u32[]{:S(2)}, u32[]{:S(2)}) collective-permute-start(f32[2,25,128]{2,1,0:T(8,128)S(1)} %get-tuple-element.32), channel_id=1, source_target_pairs={{0,4},{1,5},{2,6},{3,7},{8,12},{9,13},{10,14},{11,15},{16,20},{17,... | collective-permute-start | bytes 76808 | tf_op jit(solution)/shard_map/ppermute | solution.py:24
  163.2 4.2 %collective-permute-done.26 = f32[2,25,128]{2,1,0:T(8,128)S(1)} collective-permute-done((f32[2,25,128]{2,1,0:T(8,128)S(1)}, f32[2,25,128]{2,1,0:T(8,128)S(1)}, u32[]{:S(2)}, u32[]{:S(2)}) %collective-permute-start.26) | collective-permute-done | bytes 25632 | tf_op jit(solution)/shard_map/ppermute | solution.py:26
  175.6 6.5 %collective-permute-done.29 = f32[1,512,128]{2,1,0:T(8,128)S(1)} collective-permute-done((f32[1,512,128]{2,1,0:T(8,128)S(1)}, f32[1,512,128]{2,1,0:T(8,128)S(1)}, u32[]{:S(2)}, u32[]{:S(2)}) %collective-permute-start.29) | collective-permute-done | bytes 262176 | tf_op jit(solution)/shard_map/ppermute | solution.py:36
  184.9 10.4 %all-reduce.3 = (f32[]{:T(128)}, f32[]{:T(128)}) all-reduce(f32[]{:T(128)S(6)} %add.145, f32[]{:T(128)} %get-tuple-element.22), channel_id=1, replica_groups=mesh['layer'=4,'row'=2,'col'=4] {'layer'}, use_global_device_ids=true, to_apply=%region_16.17 | all-reduce | flops 2 | bytes 16 | tf_op jit(solution)/shard_map/psum | solution.py:113
  195.4 12.4 %all-reduce = (f32[]{:T(128)}, f32[]{:T(128)}) all-reduce(f32[]{:T(128)} %get-tuple-element.10, f32[]{:T(128)} %get-tuple-element.11), channel_id=1, replica_groups=mesh['layer'=4,'row'=2,'col'=4] {'row','col'}, use_global_device_ids=true, to_apply=%region_17.18 | all-reduce | flops 2 | bytes 16 | tf_op jit(solution)/shard_map/psum | solution.py:113
  (111 shorter events, 55.9 us)
Async XLA Ops:
  1.4 11.0 %collective-permute-start = (f32[2,25,128]{2,1,0:T(8,128)S(1)}, f32[2,25,128]{2,1,0:T(8,128)S(1)}, u32[]{:S(2)}, u32[]{:S(2)}) collective-permute-start(f32[2,25,128]{2,1,0:T(8,128)S(1)} %get-tuple-element.62), channel_id=1, source_target_pairs={{0,4},{1,5},{2,6},{3,7},{8,12},{9,13},{10,14},{11,15},{16,20},{17,... | collective-permute-start | bytes 76808 | tf_op jit(solution)/shard_map/ppermute | solution.py:24
  6.3 6.2 %collective-permute-start.1 = (f32[2,25,128]{2,1,0:T(8,128)S(1)}, f32[2,25,128]{2,1,0:T(8,128)S(1)}, u32[]{:S(2)}, u32[]{:S(2)}) collective-permute-start(f32[2,25,128]{2,1,0:T(8,128)S(1)} %get-tuple-element.63), channel_id=1, source_target_pairs={{4,0},{5,1},{6,2},{7,3},{12,8},{13,9},{14,10},{15,11},{20,16},{21,... | collective-permute-start | bytes 76808 | tf_op jit(solution)/shard_map/ppermute | solution.py:26
  8.8 11.1 %collective-permute-start.4 = (f32[1,512,128]{2,1,0:T(8,128)S(1)}, f32[1,512,128]{2,1,0:T(8,128)S(1)}, u32[]{:S(2)}, u32[]{:S(2)}) collective-permute-start(f32[1,512,128]{2,1,0:T(8,128)S(1)} %get-tuple-element.58), channel_id=1, source_target_pairs={{0,8},{8,16},{16,24},{1,9},{9,17},{17,25},{2,10},{10,18},{18,26},{... | collective-permute-start | bytes 786440 | tf_op jit(solution)/shard_map/ppermute | solution.py:36
  14.9 5.0 %collective-permute-start.3 = (f32[2,512,25]{1,2,0:T(8,128)S(1)}, f32[2,512,25]{1,2,0:T(8,128)S(1)}, u32[]{:S(2)}, u32[]{:S(2)}) collective-permute-start(f32[2,512,25]{1,2,0:T(8,128)S(1)} %get-tuple-element.61), channel_id=1, source_target_pairs={{1,0},{2,1},{3,2},{5,4},{6,5},{7,6},{9,8},{10,9},{11,10},{13,12},{... | collective-permute-start | bytes 307208 | tf_op jit(solution)/shard_map/ppermute | solution.py:26
  22.5 6.1 %collective-permute-start.5 = (f32[2,25,128]{2,1,0:T(8,128)S(1)}, f32[2,25,128]{2,1,0:T(8,128)S(1)}, u32[]{:S(2)}, u32[]{:S(2)}) collective-permute-start(f32[2,25,128]{2,1,0:T(8,128)S(1)} %get-tuple-element.56), channel_id=1, source_target_pairs={{0,4},{1,5},{2,6},{3,7},{8,12},{9,13},{10,14},{11,15},{16,20},{17,... | collective-permute-start | bytes 76808 | tf_op jit(solution)/shard_map/ppermute | solution.py:24
  27.0 5.8 %collective-permute-start.6 = (f32[2,25,128]{2,1,0:T(8,128)S(1)}, f32[2,25,128]{2,1,0:T(8,128)S(1)}, u32[]{:S(2)}, u32[]{:S(2)}) collective-permute-start(f32[2,25,128]{2,1,0:T(8,128)S(1)} %get-tuple-element.57), channel_id=1, source_target_pairs={{4,0},{5,1},{6,2},{7,3},{12,8},{13,9},{14,10},{15,11},{20,16},{21,... | collective-permute-start | bytes 76808 | tf_op jit(solution)/shard_map/ppermute | solution.py:26
  33.8 6.7 %collective-permute-start.7 = (f32[2,512,25]{1,2,0:T(8,128)S(1)}, f32[2,512,25]{1,2,0:T(8,128)S(1)}, u32[]{:S(2)}, u32[]{:S(2)}) collective-permute-start(f32[2,512,25]{1,2,0:T(8,128)S(1)} %get-tuple-element.54), channel_id=1, source_target_pairs={{0,1},{1,2},{2,3},{4,5},{5,6},{6,7},{8,9},{9,10},{10,11},{12,13},{... | collective-permute-start | bytes 307208 | tf_op jit(solution)/shard_map/ppermute | solution.py:24
  39.2 12.8 %collective-permute-start.9 = (f32[1,512,128]{2,1,0:T(8,128)S(1)}, f32[1,512,128]{2,1,0:T(8,128)S(1)}, u32[]{:S(2)}, u32[]{:S(2)}) collective-permute-start(f32[1,512,128]{2,1,0:T(8,128)S(1)} %get-tuple-element.49), channel_id=1, source_target_pairs={{8,0},{16,8},{24,16},{9,1},{17,9},{25,17},{10,2},{18,10},{26,18},{... | collective-permute-start | bytes 786440 | tf_op jit(solution)/shard_map/ppermute | solution.py:36
  45.2 5.8 %collective-permute-start.11 = (f32[2,25,128]{2,1,0:T(8,128)S(1)}, f32[2,25,128]{2,1,0:T(8,128)S(1)}, u32[]{:S(2)}, u32[]{:S(2)}) collective-permute-start(f32[2,25,128]{2,1,0:T(8,128)S(1)} %get-tuple-element.53), channel_id=1, source_target_pairs={{4,0},{5,1},{6,2},{7,3},{12,8},{13,9},{14,10},{15,11},{20,16},{21,... | collective-permute-start | bytes 76808 | tf_op jit(solution)/shard_map/ppermute | solution.py:26
  52.9 35.9 %collective-permute-start.14 = (f32[1,512,128]{2,1,0:T(8,128)S(1)}, f32[1,512,128]{2,1,0:T(8,128)S(1)}, u32[]{:S(2)}, u32[]{:S(2)}) collective-permute-start(f32[1,512,128]{2,1,0:T(8,128)S(1)} %get-tuple-element.46), channel_id=1, source_target_pairs={{0,8},{8,16},{16,24},{1,9},{9,17},{17,25},{2,10},{10,18},{18,26},{... | collective-permute-start | bytes 786440 | tf_op jit(solution)/shard_map/ppermute | solution.py:36
  57.1 31.6 %collective-permute-start.12 = (f32[2,512,25]{1,2,0:T(8,128)}, f32[2,512,25]{1,2,0:T(8,128)}, u32[]{:S(2)}, u32[]{:S(2)}) collective-permute-start(f32[2,512,25]{1,2,0:T(8,128)} %get-tuple-element.50), channel_id=1, source_target_pairs={{0,1},{1,2},{2,3},{4,5},{5,6},{6,7},{8,9},{9,10},{10,11},{12,13},{... | collective-permute-start | bytes 307208 | tf_op jit(solution)/shard_map/ppermute | solution.py:24
  61.8 26.9 %collective-permute-start.13 = (f32[2,512,25]{1,2,0:T(8,128)}, f32[2,512,25]{1,2,0:T(8,128)}, u32[]{:S(2)}, u32[]{:S(2)}) collective-permute-start(f32[2,512,25]{1,2,0:T(8,128)} %get-tuple-element.51), channel_id=1, source_target_pairs={{1,0},{2,1},{3,2},{5,4},{6,5},{7,6},{9,8},{10,9},{11,10},{13,12},{... | collective-permute-start | bytes 307208 | tf_op jit(solution)/shard_map/ppermute | solution.py:26
  93.4 4.8 %collective-permute-start.15 = (f32[2,25,128]{2,1,0:T(8,128)S(1)}, f32[2,25,128]{2,1,0:T(8,128)S(1)}, u32[]{:S(2)}, u32[]{:S(2)}) collective-permute-start(f32[2,25,128]{2,1,0:T(8,128)S(1)} %get-tuple-element.44), channel_id=1, source_target_pairs={{0,4},{1,5},{2,6},{3,7},{8,12},{9,13},{10,14},{11,15},{16,20},{17,... | collective-permute-start | bytes 76808 | tf_op jit(solution)/shard_map/ppermute | solution.py:24
  96.6 5.8 %collective-permute-start.16 = (f32[2,25,128]{2,1,0:T(8,128)S(1)}, f32[2,25,128]{2,1,0:T(8,128)S(1)}, u32[]{:S(2)}, u32[]{:S(2)}) collective-permute-start(f32[2,25,128]{2,1,0:T(8,128)S(1)} %get-tuple-element.45), channel_id=1, source_target_pairs={{4,0},{5,1},{6,2},{7,3},{12,8},{13,9},{14,10},{15,11},{20,16},{21,... | collective-permute-start | bytes 76808 | tf_op jit(solution)/shard_map/ppermute | solution.py:26
  103.4 4.1 %collective-permute-start.17 = (f32[2,512,25]{1,2,0:T(8,128)S(1)}, f32[2,512,25]{1,2,0:T(8,128)S(1)}, u32[]{:S(2)}, u32[]{:S(2)}) collective-permute-start(f32[2,512,25]{1,2,0:T(8,128)S(1)} %get-tuple-element.42), channel_id=1, source_target_pairs={{0,1},{1,2},{2,3},{4,5},{5,6},{6,7},{8,9},{9,10},{10,11},{12,13},{... | collective-permute-start | bytes 307208 | tf_op jit(solution)/shard_map/ppermute | solution.py:24
  106.2 12.0 %collective-permute-start.19 = (f32[1,512,128]{2,1,0:T(8,128)S(1)}, f32[1,512,128]{2,1,0:T(8,128)S(1)}, u32[]{:S(2)}, u32[]{:S(2)}) collective-permute-start(f32[1,512,128]{2,1,0:T(8,128)S(1)} %get-tuple-element.37), channel_id=1, source_target_pairs={{8,0},{16,8},{24,16},{9,1},{17,9},{25,17},{10,2},{18,10},{26,18},{... | collective-permute-start | bytes 786440 | tf_op jit(solution)/shard_map/ppermute | solution.py:36
  111.4 5.8 %collective-permute-start.21 = (f32[2,25,128]{2,1,0:T(8,128)S(1)}, f32[2,25,128]{2,1,0:T(8,128)S(1)}, u32[]{:S(2)}, u32[]{:S(2)}) collective-permute-start(f32[2,25,128]{2,1,0:T(8,128)S(1)} %get-tuple-element.41), channel_id=1, source_target_pairs={{4,0},{5,1},{6,2},{7,3},{12,8},{13,9},{14,10},{15,11},{20,16},{21,... | collective-permute-start | bytes 76808 | tf_op jit(solution)/shard_map/ppermute | solution.py:26
  119.1 34.7 %collective-permute-start.24 = (f32[1,512,128]{2,1,0:T(8,128)S(1)}, f32[1,512,128]{2,1,0:T(8,128)S(1)}, u32[]{:S(2)}, u32[]{:S(2)}) collective-permute-start(f32[1,512,128]{2,1,0:T(8,128)S(1)} %get-tuple-element.34), channel_id=1, source_target_pairs={{0,8},{8,16},{16,24},{1,9},{9,17},{17,25},{2,10},{10,18},{18,26},{... | collective-permute-start | bytes 786440 | tf_op jit(solution)/shard_map/ppermute | solution.py:36
  124.0 29.8 %collective-permute-start.22 = (f32[2,512,25]{1,2,0:T(8,128)}, f32[2,512,25]{1,2,0:T(8,128)}, u32[]{:S(2)}, u32[]{:S(2)}) collective-permute-start(f32[2,512,25]{1,2,0:T(8,128)} %get-tuple-element.38), channel_id=1, source_target_pairs={{0,1},{1,2},{2,3},{4,5},{5,6},{6,7},{8,9},{9,10},{10,11},{12,13},{... | collective-permute-start | bytes 307208 | tf_op jit(solution)/shard_map/ppermute | solution.py:24
  126.6 27.2 %collective-permute-start.23 = (f32[2,512,25]{1,2,0:T(8,128)}, f32[2,512,25]{1,2,0:T(8,128)}, u32[]{:S(2)}, u32[]{:S(2)}) collective-permute-start(f32[2,512,25]{1,2,0:T(8,128)} %get-tuple-element.39), channel_id=1, source_target_pairs={{1,0},{2,1},{3,2},{5,4},{6,5},{7,6},{9,8},{10,9},{11,10},{13,12},{... | collective-permute-start | bytes 307208 | tf_op jit(solution)/shard_map/ppermute | solution.py:26
  158.4 4.8 %collective-permute-start.25 = (f32[2,25,128]{2,1,0:T(8,128)S(1)}, f32[2,25,128]{2,1,0:T(8,128)S(1)}, u32[]{:S(2)}, u32[]{:S(2)}) collective-permute-start(f32[2,25,128]{2,1,0:T(8,128)S(1)} %get-tuple-element.32), channel_id=1, source_target_pairs={{0,4},{1,5},{2,6},{3,7},{8,12},{9,13},{10,14},{11,15},{16,20},{17,... | collective-permute-start | bytes 76808 | tf_op jit(solution)/shard_map/ppermute | solution.py:24
  161.7 5.8 %collective-permute-start.26 = (f32[2,25,128]{2,1,0:T(8,128)S(1)}, f32[2,25,128]{2,1,0:T(8,128)S(1)}, u32[]{:S(2)}, u32[]{:S(2)}) collective-permute-start(f32[2,25,128]{2,1,0:T(8,128)S(1)} %get-tuple-element.33), channel_id=1, source_target_pairs={{4,0},{5,1},{6,2},{7,3},{12,8},{13,9},{14,10},{15,11},{20,16},{21,... | collective-permute-start | bytes 76808 | tf_op jit(solution)/shard_map/ppermute | solution.py:26
  168.4 4.1 %collective-permute-start.27 = (f32[2,512,25]{1,2,0:T(8,128)S(1)}, f32[2,512,25]{1,2,0:T(8,128)S(1)}, u32[]{:S(2)}, u32[]{:S(2)}) collective-permute-start(f32[2,512,25]{1,2,0:T(8,128)S(1)} %get-tuple-element.30), channel_id=1, source_target_pairs={{0,1},{1,2},{2,3},{4,5},{5,6},{6,7},{8,9},{9,10},{10,11},{12,13},{... | collective-permute-start | bytes 307208 | tf_op jit(solution)/shard_map/ppermute | solution.py:24
  171.2 10.9 %collective-permute-start.29 = (f32[1,512,128]{2,1,0:T(8,128)S(1)}, f32[1,512,128]{2,1,0:T(8,128)S(1)}, u32[]{:S(2)}, u32[]{:S(2)}) collective-permute-start(f32[1,512,128]{2,1,0:T(8,128)S(1)} %get-tuple-element.29), channel_id=1, source_target_pairs={{8,0},{16,8},{24,16},{9,1},{17,9},{25,17},{10,2},{18,10},{26,18},{... | collective-permute-start | bytes 786440 | tf_op jit(solution)/shard_map/ppermute | solution.py:36
  (22 other events, 135.2 us)
